TPU v7x, 32 devices: a whole 2x2x4 slice. The times are simulated.
32 devices in a mesh: dp: 4 (over z), expert: 4 (over y, x), tensor: 2 (over core).
Axes of the slice: x: 2, y: 2, z: 4, core: 2. Of those that a mesh axis runs over, the one named last changes fastest.
Arguments:
- tokens: bfloat16 [512, 6144], P('dp'), may hold values from -6 to 6
- norm_gain: float32 [6144], replicated, may hold values from 0.1 to 1.9
- expert_ids: int32 [512, 2], P('dp'), may hold values from 0 to 3, all different within a row; in each aligned block of 128 rows (0 to 127, 128 to 255, ...) at most 72 rows name the same one
- gate_weights: float32 [512, 2], P('dp'), may hold values from 0.1 to 0.9
- w_gate: bfloat16 [4, 6144, 12288], P('expert', None, ('dp', 'tensor')), may hold values from -0.078125 to 0.078125
- w_up: bfloat16 [4, 6144, 12288], P('expert', None, ('dp', 'tensor')), may hold values from -0.078125 to 0.078125
- w_down: bfloat16 [4, 12288, 6144], P('expert', 'dp', 'tensor'), may hold values from -0.0546875 to 0.0546875
- label_rows: bfloat16 [512, 6144], P(('dp', 'expert'), 'tensor'), may hold values from -4 to 4, as said below
- seg_ids: int32 [4, 128], P('dp'), may hold values from 0 to 3, never falling along the last dimension, each value on 1 to 64 neighbouring positions
- pair_slot: int32 [4, 4], P('dp'), may hold values from 0 to 3, each once within a row
- ref_scores: float32 [4, 4], P('dp'), may hold values from -8 to 8
Outputs:
- layer_out: bfloat16 [512, 6144], P(('dp', 'expert'), 'tensor')
- margins: float32 [4, 2], P('dp')
Inputs may be any that keep to these rules, and one draw needn't show every extreme that they name: `expert_ids`: each row names two different experts. Among the 128 rows of one dp group no expert is named more than 72 times, and in some group some expert is named exactly 72 times. `seg_ids`: within each row sequence numbers never fall; every sequence has 1 to 64 tokens and one has exactly 64. `pair_slot`: each row holds every number of 0 to 3 once. `label_rows`: entries lie within 27 / sqrt(6144) in magnitude.
All inputs are finite; a program needn't handle non-finite values.
Results may differ from a plain program's by a relative error of at most 0.009.
Values may be sent and summed in bfloat16 or wider, within the bound.
A program may use at most 128 MiB of HBM per device.

v0:
```python
import jax
import jax.numpy as jnp
from jax import lax
from jax.sharding import PartitionSpec as P

SEQS = 4
PAIRS = 2


epsilon = 1e-05
dpo_beta = 0.5


def normed_rows(tokens, norm_gain):
    values = tokens.astype(jnp.float32)
    inverse_rms = lax.rsqrt(jnp.mean(values * values, axis=1, keepdims=True) + epsilon)
    return (values * inverse_rms * norm_gain[None, :]).astype(jnp.bfloat16)


def slot_tables(expert_ids, gate_weights, experts, capacity):
    tok_count = expert_ids.shape[0]
    flat_ids = expert_ids.reshape(-1)
    onehot = (flat_ids[:, None] == jnp.arange(experts, dtype=jnp.int32)[None, :]).astype(jnp.int32)
    earlier = jnp.cumsum(onehot, axis=0) - onehot
    position = jnp.sum(earlier * onehot, axis=1)
    slot_index = flat_ids * capacity + position
    slot_match = (
        slot_index[:, None] == jnp.arange(experts * capacity, dtype=jnp.int32)[None, :]
    ).astype(jnp.float32)
    slot_match = slot_match.reshape(tok_count, 2, experts * capacity)
    placement = jnp.sum(slot_match, axis=1)
    mixing = jnp.sum(slot_match * gate_weights[:, :, None], axis=1)
    return (placement, mixing)


def body(
    tokens,
    norm_gain,
    expert_ids,
    gate_weights,
    w_gate,
    w_up,
    w_down,
    label_rows,
    seg_ids,
    pair_slot,
    ref_scores,
):
    group_count = tokens.shape[0]
    experts = lax.axis_size("expert")
    expert_index = lax.axis_index("expert")
    capacity = max(2, 9 * group_count // (4 * experts))
    tensor_count = lax.axis_size("tensor")
    column_width = tokens.shape[1] // tensor_count
    tensor_index = lax.axis_index("tensor")
    own_count = group_count // experts
    normed = normed_rows(tokens, norm_gain)
    placement, mixing = slot_tables(expert_ids, gate_weights, experts, capacity)
    own_place = lax.dynamic_slice_in_dim(placement, expert_index * capacity, capacity, 1)
    own_mixing = lax.dynamic_slice_in_dim(mixing, expert_index * capacity, capacity, 1)
    arrived = jnp.dot(
        own_place.T.astype(jnp.bfloat16), normed, preferred_element_type=jnp.float32
    ).astype(jnp.bfloat16)
    gate_local = w_gate[0]
    up_local = w_up[0]
    down_local = w_down[0]
    own_columns = lax.dynamic_slice_in_dim(arrived, tensor_index * column_width, column_width, 1)
    group_rows = lax.all_gather(own_columns, "dp", axis=0, tiled=True)
    block_cols = lax.all_gather(group_rows, "tensor", axis=1, tiled=True)
    gate_sum = jnp.dot(block_cols, gate_local, preferred_element_type=jnp.float32)
    up_sum = jnp.dot(block_cols, up_local, preferred_element_type=jnp.float32)
    hidden = (jax.nn.silu(gate_sum) * up_sum).astype(jnp.bfloat16)
    hidden_block = lax.all_gather(hidden, "tensor", axis=1, tiled=True)
    own_rows = lax.psum_scatter(
        jnp.dot(hidden_block, down_local, preferred_element_type=jnp.float32).astype(jnp.bfloat16),
        "dp",
        scatter_dimension=0,
        tiled=True,
    )
    weighted = jnp.dot(own_mixing, own_rows.astype(jnp.float32), precision=lax.Precision.HIGHEST)
    expert_mix = lax.psum_scatter(
        weighted.astype(jnp.bfloat16), "expert", scatter_dimension=0, tiled=True
    ).astype(jnp.float32)
    token_rows = lax.dynamic_slice_in_dim(tokens, expert_index * own_count, own_count, 0)
    residual = lax.dynamic_slice_in_dim(
        token_rows, tensor_index * column_width, column_width, 1
    ).astype(jnp.float32)
    mixed = residual + expert_mix
    layer_out = mixed.astype(jnp.bfloat16)
    token_score = jnp.sum(mixed * label_rows.astype(jnp.float32), axis=1)
    sequence_ids = lax.dynamic_slice_in_dim(seg_ids[0], expert_index * own_count, own_count, 0)
    member = (sequence_ids[:, None] == jnp.arange(SEQS, dtype=jnp.int32)[None, :]).astype(
        jnp.float32
    )
    partial_value = jnp.sum(member * token_score[:, None], axis=0)
    totals = lax.psum(partial_value, ("expert", "tensor"))
    slots_here = pair_slot[0]
    polarity = (1 - 2 * (slots_here % 2)).astype(jnp.float32)
    pair_member = (
        (slots_here // 2)[:, None] == jnp.arange(PAIRS, dtype=jnp.int32)[None, :]
    ).astype(jnp.float32)
    margins = dpo_beta * jnp.sum(
        pair_member * (polarity * (totals - ref_scores[0]))[:, None], axis=0
    )
    return (layer_out, margins[None, :])


def solution(mesh):
    placed = (
        P("dp", None),
        P(),
        P("dp", None),
        P("dp", None),
        P("expert", None, ("dp", "tensor")),
        P("expert", None, ("dp", "tensor")),
        P("expert", "dp", "tensor"),
        P(("dp", "expert"), "tensor"),
        P("dp", None),
        P("dp", None),
        P("dp", None),
    )
    return jax.shard_map(
        body,
        mesh=mesh,
        in_specs=placed,
        out_specs=(P(("dp", "expert"), "tensor"), P("dp", None)),
        check_vma=False,
    )
```

profile of v0, /device:TPU:0, one launch (start us, length us, event | category | flops | bytes accessed | tf_op | source)
XLA Modules:
  0.0 209.0 jit_solution(1095833018729671077)
XLA Ops:
  7.2 0.0 copy-start
  7.2 0.0 all-gather.4.cloned.1.call-start
  7.2 0.8 copy.31
  8.0 0.1 eq.73
  8.2 0.1 eq.69
  8.3 1.2 reduce-window.6
  9.5 0.1 slice.8
  9.6 0.1 copy.33
  9.8 0.1 copy.34
  9.9 0.1 add_bitcast_fusion
  10.0 0.1 reduce_sum.66
  10.1 0.1 copy.35
  10.2 0.7 multiply_add_fusion
  10.9 1.8 fusion.9
  12.7 0.8 select_reduce_fusion
  13.4 2.1 %fusion.18 = bf16[72,6144]{1,0:T(8,128)(2,1)S(1)} fusion(bf16[128,6144]{1,0:T(8,128)(2,1)} %param.11, f32[6144]{0:T(1024)} %param.12, f32[128]{0:T(128)S(1)} %add_rsqrt_fusion, bf16[128,288]{0,1:T(8,128)(2,1)S(1)} %get-tuple-element.3, s32[]{:T(128)S(6)} %select_n.36), kind=kOutput, calls=%fused_computation.15 | convolution fusion | flops 116391936 | bytes 2501124 | tf_op jit(solution)/shard_map/dot_general | solution.py:61
  15.5 0.8 dynamic-slice_convert_fusion
  16.4 0.0 all-gather.4.cloned.1.call-update
  16.4 0.0 all-gather.6.cloned.1.call-start
  16.4 43.1 %all-gather.4.cloned.1.call-done = bf16[288,3072]{1,0:T(8,128)(2,1)} async-done(((bf16[72,3072]{1,0:T(8,128)(2,1)}), bf16[288,3072]{1,0:T(8,128)(2,1)}) %all-gather.4.cloned.1.call-update) | async-done | bytes 1769488 | tf_op jit(solution)/shard_map/all_gather | solution.py:68
  59.5 0.0 all-gather.6.cloned.1.call-update
  59.5 0.0 all-gather.8.cloned.1.call-start
  59.6 13.0 %all-gather.6.cloned.1.call-done = bf16[288,6144]{1,0:T(8,128)(2,1)} async-done(((bf16[288,3072]{1,0:T(8,128)(2,1)}), bf16[288,6144]{1,0:T(8,128)(2,1)}) %all-gather.6.cloned.1.call-update) | async-done | bytes 3538960 | tf_op jit(solution)/shard_map/all_gather | solution.py:69
  72.6 0.0 copy-start.4
  72.6 13.2 %fusion.4 = f32[288,1536]{1,0:T(8,128)S(1)} fusion(bf16[288,6144]{1,0:T(8,128)(2,1)} %all-gather.6.cloned.1.call-done, bf16[1,6144,1536]{2,1,0:T(8,128)(2,1)} %param.15), kind=kOutput, calls=%fused_computation.4 | convolution fusion | flops 5435817984 | bytes 24182784 | tf_op jit(solution)/shard_map/dot_general | solution.py:70
  85.8 0.0 copy-done.4
  85.8 11.0 %fusion.15 = bf16[288,1536]{1,0:T(8,128)(2,1)} fusion(bf16[288,6144]{1,0:T(8,128)(2,1)S(1)} %copy-done.4, bf16[1,6144,1536]{2,1,0:T(8,128)(2,1)} %param.16, f32[288,1536]{1,0:T(8,128)S(1)} %fusion.4), kind=kOutput, calls=%fused_computation.14 | convolution fusion | flops 5438472192 | bytes 25067520 | tf_op jit(solution)/shard_map/dot_general | solution.py:71
  96.8 0.0 all-gather.8.cloned.1.call-update
  96.8 0.0 reduce-scatter.3.cloned.1.call-start
  96.9 11.4 %all-gather.8.cloned.1.call-done = bf16[288,3072]{1,0:T(8,128)(2,1)} async-done(((bf16[288,1536]{1,0:T(8,128)(2,1)}), bf16[288,3072]{1,0:T(8,128)(2,1)}) %all-gather.8.cloned.1.call-update) | async-done | bytes 1769488 | tf_op jit(solution)/shard_map/all_gather | solution.py:73
  108.3 11.1 %fusion.6 = bf16[288,3072]{1,0:T(8,128)(2,1)} fusion(bf16[288,3072]{1,0:T(8,128)(2,1)} %all-gather.8.cloned.1.call-done, bf16[1,3072,3072]{2,1,0:T(8,128)(2,1)} %param.17), kind=kOutput, calls=%fused_computation.6 | convolution fusion | flops 5436702720 | bytes 22413312 | tf_op jit(solution)/shard_map/dot_general | solution.py:75
  119.4 0.0 copy-start.1
  119.4 0.0 copy-start.3
  119.4 0.0 copy-start.2
  119.4 0.0 reduce-scatter.3.cloned.1.call-update
  119.4 0.0 reduce-scatter.5.cloned.1.call-start
  119.4 39.8 %reduce-scatter.3.cloned.1.call-done = bf16[72,3072]{1,0:T(8,128)(2,1)} async-done(((bf16[288,3072]{1,0:T(8,128)(2,1)}), bf16[72,3072]{1,0:T(8,128)(2,1)}) %reduce-scatter.3.cloned.1.call-update) | async-done | bytes 442384 | tf_op jit(solution)/shard_map/reduce_scatter | solution.py:74
  159.2 2.7 %convolution_convert_fusion = bf16[128,3072]{1,0:T(8,128)(2,1)} fusion(bf16[72,3072]{1,0:T(8,128)(2,1)} %reduce-scatter.3.cloned.1.call-done, f32[128,288]{0,1:T(8,128)S(1)} %get-tuple-element.2, s32[]{:T(128)S(6)} %select_n.36), kind=kOutput, calls=%fused_computation.9 | convolution fusion | flops 340131840 | bytes 1265668 | tf_op jit(solution)/shard_map/dot_general | solution.py:80
  161.9 0.0 reduce-scatter.5.cloned.1.call-update
  161.9 0.0 copy-done
  162.0 0.1 fusion.30
  162.0 25.2 %reduce-scatter.5.cloned.1.call-done = bf16[32,3072]{1,0:T(8,128)(2,1)} async-done(((bf16[128,3072]{1,0:T(8,128)(2,1)}), bf16[32,3072]{1,0:T(8,128)(2,1)}) %reduce-scatter.5.cloned.1.call-update) | async-done | bytes 196624 | tf_op jit(solution)/shard_map/reduce_scatter | solution.py:81
  187.2 0.0 copy-done.1
  187.2 2.0 multiply_reduce_fusion
  189.2 0.1 select_reduce_fusion.1
  189.3 0.0 copy-done.3
  189.4 12.5 %psum.7 = f32[4]{0:T(128)S(1)} all-reduce(f32[4]{0:T(128)S(1)} %select_reduce_fusion.1), channel_id=1, replica_groups=mesh['dp'=4,'expert'=4,'tensor'=2] {'expert','tensor'}, use_global_device_ids=true, to_apply=%region_10.11 | all-reduce | flops 4 | bytes 32 | tf_op jit(solution)/shard_map/psum | solution.py:96
  201.8 0.0 copy-done.2
  201.8 0.1 fusion.27
  201.9 0.5 multiply_bitcast_fusion
  (7 shorter events, 0.1 us)
Async XLA Ops:
  7.2 154.8 %copy-start = (s32[1,128]{1,0:T(1,128)S(1)}, s32[1,128]{1,0:T(1,128)}, u32[]{:S(2)}) copy-start(s32[1,128]{1,0:T(1,128)} %param.19) | copy-start | bytes 1540
  7.2 52.3 %all-gather.4.cloned.1.call-start = ((), (), s32[]{:S(2)}) async-start(), calls=%async_computation.2 | async-start | bytes 2211840 | tf_op jit(solution)/shard_map/all_gather | solution.py:68
  16.4 56.2 %all-gather.6.cloned.1.call-start = ((), (), s32[]{:S(2)}) async-start(), calls=%async_computation.3 | async-start | bytes 5308416 | tf_op jit(solution)/shard_map/all_gather | solution.py:69
  59.5 48.7 %all-gather.8.cloned.1.call-start = ((), (), s32[]{:S(2)}) async-start(), calls=%async_computation.4 | async-start | bytes 2654208 | tf_op jit(solution)/shard_map/all_gather | solution.py:73
  72.6 13.2 %copy-start.4 = (bf16[288,6144]{1,0:T(8,128)(2,1)S(1)}, bf16[288,6144]{1,0:T(8,128)(2,1)}, u32[]{:S(2)}) copy-start(bf16[288,6144]{1,0:T(8,128)(2,1)} %all-gather.6.cloned.1.call-done) | copy-start | bytes 10616836
  96.8 62.4 %reduce-scatter.3.cloned.1.call-start = ((), (), s32[]{:S(2)}) async-start(), calls=%async_computation.5 | async-start | bytes 2211840 | tf_op jit(solution)/shard_map/reduce_scatter | solution.py:74
  119.4 67.9 %copy-start.1 = (bf16[32,3072]{1,0:T(8,128)(2,1)S(1)}, bf16[32,3072]{1,0:T(8,128)(2,1)}, u32[]{:S(2)}) copy-start(bf16[32,3072]{1,0:T(8,128)(2,1)} %param.18) | copy-start | bytes 589828
  119.4 70.0 %copy-start.3 = (s32[1,4]{1,0:T(1,128)S(1)}, s32[1,4]{1,0:T(1,128)}, u32[]{:S(2)}) copy-start(s32[1,4]{1,0:T(1,128)} %param.20) | copy-start | bytes 52
  119.4 82.5 %copy-start.2 = (f32[1,4]{1,0:T(1,128)S(1)}, f32[1,4]{1,0:T(1,128)}, u32[]{:S(2)}) copy-start(f32[1,4]{1,0:T(1,128)} %param.21) | copy-start | bytes 52
  119.4 67.8 %reduce-scatter.5.cloned.1.call-start = ((), (), s32[]{:S(2)}) async-start(), calls=%async_computation.6 | async-start | bytes 983040 | tf_op jit(solution)/shard_map/reduce_scatter | solution.py:81
Sparse Core Ops, SparseCore 0:
  16.5 42.9 all-gather.3
  61.1 11.5 all-gather.5
  97.0 11.2 all-gather.7
  119.5 39.6 reduce-scatter.2
  162.1 25.1 reduce-scatter.4
where the time goes:
time: 209 us
  waiting for transfers between devices  133 us (64%)
  matrix products  40.1 us (19%)
  between operations  13.9 us (7%)
  blocking collectives  12.5 us (6%)
  other arithmetic  7.38 us (4%)
  local copies, waits for them, and re-layouts  2.45 us (1%)
    all_gather x1, waiting for transfers between devices, body(): group_rows = lax.all_gather(own_columns, 'dp', axis=0, tiled=True)  43.1 us
    reduce_scatter x1, waiting for transfers between devices, body(): lax.psum_scatter(jnp.dot(hidden_block, down_local, preferred_element_type...  39.8 us
    reduce_scatter x1, waiting for transfers between devices, body(): lax.psum_scatter(weighted.astype(jnp.bfloat16), 'expert', scatter_dimensi...  25.2 us
    dot_general x1, matrix products, body(): jnp.dot(block_cols, gate_local, preferred_element_type=jnp.float32)  13.2 us
    all_gather x1, waiting for transfers between devices, body(): block_cols = lax.all_gather(group_rows, 'tensor', axis=1, tiled=True)  13 us
    psum x1, blocking collectives, body(): totals = lax.psum(partial_value, ('expert', 'tensor'))  12.5 us
    all_gather x1, waiting for transfers between devices, body(): hidden_block = lax.all_gather(hidden, 'tensor', axis=1, tiled=True)  11.4 us
    dot_general x1, matrix products, body(): jnp.dot(hidden_block, down_local, preferred_element_type=jnp.float32)  11.1 us
  transfers between devices with their start and end apart: 5, of which 5 were waited for; matrix products, arithmetic and copies ran while one was open for 0% of the time, Pallas kernels for 0%

commit v1 on v0

v1 whole, which is shorter than its diff:
```python
import functools

import jax
import jax.numpy as jnp
from jax import lax
from jax.experimental import pallas as pl
from jax.experimental.pallas import tpu as pltpu
from jax.sharding import PartitionSpec as P

SEQS = 4
PAIRS = 2
LANES = 128
epsilon = 1e-05
dpo_beta = 0.5
F32 = jnp.float32
BF16 = jnp.bfloat16
MESH = pl.DeviceIdType.MESH


def dims(mesh_shape, group, width, hidden):
    dp, ex, tn = mesh_shape
    cap = max(2, 9 * group // (4 * ex))
    cap_pad = -(-cap // 16) * 16
    piece = width // (ex * tn)
    chunks = 3 if piece % 384 == 0 else 1
    sub = piece // chunks
    h_tile = 256 if hidden % 256 == 0 else 128
    p_tile = 256 if piece % 256 == 0 else 128
    return dp, ex, tn, cap_pad, piece, chunks, sub, h_tile, p_tile


def kernel(
    size, tokens, gain, meta_in, label, member, w_gate, w_up, w_down,
    out, totals,
    normed, meta, tok, pack, rows, wg, wu, wd, acc_g, acc_u, hid, dn_out, dn_in,
    mix_out, mix_in, tr_out, tr_in, sc_out, sc_in,
    w_sem, d_sem, meta_s, meta_r, z_s, z_r, x_s, x_r, f_s, f_r, h_s, h_r,
    n_s, n_r, m_s, m_r, t_s, t_r, c_s, c_r,
):
    dp, ex, tn, cap, piece, chunks, sub, h_tile, p_tile = size
    group, width = tokens.shape
    half = width // tn
    hidden = w_gate.shape[2]
    depth = ex * tn * sub
    count = group // ex
    g, e, t = lax.axis_index("dp"), lax.axis_index("expert"), lax.axis_index("tensor")
    slots = min(chunks, 2)
    d_slots = wd.shape[0]
    sent = []

    def at_dp(k):
        return (lax.rem(g + k, dp), e, t)

    def at_ex(k):
        return (g, lax.rem(e + k, ex), t)

    def at_tn(k):
        return (g, e, lax.rem(t + k, tn))

    def remote(src, dst, s, r, dev):
        return pltpu.make_async_remote_copy(
            src_ref=src, dst_ref=dst, send_sem=s, recv_sem=r, device_id=dev, device_id_type=MESH
        )

    def send(*a):
        c = remote(*a)
        c.start()
        sent.append(c)

    def load_chunk(s):
        for i, (src, dst) in enumerate(((w_gate, wg), (w_up, wu))):
            for q in range(ex * tn):
                pltpu.make_async_copy(
                    src.at[0, pl.ds(q * piece + s * sub, sub)],
                    dst.at[s % slots, pl.ds(q * sub, sub)],
                    w_sem.at[i, s],
                ).start()

    def wait_chunk(s):
        for i, (src, dst) in enumerate(((w_gate, wg), (w_up, wu))):
            pltpu.make_async_copy(src.at[0, pl.ds(0, depth)], dst.at[s % slots], w_sem.at[i, s]).wait()

    def down_copy(i):
        owner = lax.rem(e + i + 1, ex)
        return pltpu.make_async_copy(
            w_down.at[0, :, pl.ds(pl.multiple_of(owner * piece, LANES), piece)],
            wd.at[i % d_slots],
            d_sem.at[i],
        )

    for s in range(slots):
        load_chunk(s)
    for i in range(d_slots):
        down_copy(i).start()

    barrier = pltpu.get_barrier_semaphore()
    peers = 0
    for k in range(1, dp):
        pl.semaphore_signal(barrier, inc=1, device_id=at_dp(k), device_id_type=MESH)
        peers += 1
    for k in range(ex):
        for j in range(tn):
            if k or j:
                dev = (g, lax.rem(e + k, ex), lax.rem(t + j, tn))
                pl.semaphore_signal(barrier, inc=1, device_id=dev, device_id_type=MESH)
                peers += 1

    step = 16

    @pl.loop(0, group // step)
    def _(i):
        at = pl.ds(pl.multiple_of(i * step, step), step)
        v = tokens[at, :].astype(F32)
        inv = lax.rsqrt(jnp.mean(v * v, axis=1, keepdims=True) + epsilon)
        normed[at, :] = (v * inv * gain[...]).astype(BF16)

    info = meta_in[...]
    eid = lax.broadcasted_iota(jnp.int32, (16, group), 0).astype(F32)
    id0, id1 = info[2:3, :], info[3:4, :]
    hit0, hit1 = eid == id0, eid == id1
    named = jnp.where(hit0 | hit1, 1.0, 0.0).astype(BF16)
    tri = (
        lax.broadcasted_iota(jnp.int32, (group, group), 0)
        < lax.broadcasted_iota(jnp.int32, (group, group), 1)
    )
    earlier = jnp.dot(named, jnp.where(tri, 1.0, 0.0).astype(BF16), preferred_element_type=F32)
    pos0 = jnp.sum(jnp.where(hit0, earlier, 0.0), axis=0, keepdims=True)
    pos1 = jnp.sum(jnp.where(hit1, earlier, 0.0), axis=0, keepdims=True)
    s0, s1 = id0 * cap + pos0, id1 * cap + pos1
    r8 = lax.broadcasted_iota(jnp.int32, (8, group), 0)
    meta[0] = jnp.where(r8 == 2, s0, jnp.where(r8 == 3, s1, info))

    pl.semaphore_wait(barrier, peers)

    my_col = pl.multiple_of(t * half + e * piece, LANES)
    for k in range(1, dp):
        send(meta.at[0], meta.at[dp - k], meta_s.at[k], meta_r.at[dp - k], at_dp(k))
    for s in range(chunks):
        for k in range(1, dp):
            send(
                normed.at[:, pl.ds(pl.multiple_of(my_col + s * sub, LANES), sub)],
                tok.at[s, dp - k],
                z_s.at[s, k], z_r.at[s, dp - k], at_dp(k),
            )

    row_id = lax.broadcasted_iota(jnp.int32, (cap, group), 0).astype(F32) + (e * cap).astype(F32)
    own_hot = jnp.where((row_id == s0) | (row_id == s1), 1.0, 0.0).astype(BF16)
    for s in range(chunks):
        for q in range(ex * tn):
            rows[s, 0, :, q * sub:(q + 1) * sub] = jnp.dot(
                own_hot, normed[:, q * piece + s * sub:q * piece + (s + 1) * sub],
                preferred_element_type=F32,
            ).astype(BF16)

    all_id = lax.broadcasted_iota(jnp.int32, (ex * cap, group), 0).astype(F32)
    mine = t * ex + e

    def block(q):
        return pl.ds(pl.multiple_of(q * sub, LANES), sub)

    def forward(s, owner, k):
        for j in range(1, tn):
            ref = rows.at[s, pl.ds(1, dp - 1), :, block(t * ex + owner)]
            send(ref, ref, f_s.at[s, k, j], f_r.at[s, k, tn - j], at_tn(j))

    def pack_chunk(s):
        for d in range(1, dp):
            if s == 0:
                remote(meta.at[0], meta.at[d], meta_s.at[d], meta_r.at[d], at_dp(d)).wait_recv()
            remote(tok.at[s, d], tok.at[s, d], z_s.at[s, d], z_r.at[s, d], at_dp(d)).wait_recv()
            hot = jnp.where((all_id == meta[d, 2:3, :]) | (all_id == meta[d, 3:4, :]), 1.0, 0.0)
            got = jnp.dot(hot.astype(BF16), tok[s, d], preferred_element_type=F32)
            got = got.astype(BF16).reshape(ex, cap, sub)
            for x in range(ex):
                pack[s, x, d - 1] = got[x]
            rows[s, d, :, block(mine)] = pack[s, e, d - 1]
        for k in range(1, ex):
            send(
                pack.at[s, lax.rem(e + k, ex)],
                rows.at[s, pl.ds(1, dp - 1), :, block(mine)],
                x_s.at[s, k], x_r.at[s, ex - k], at_ex(k),
            )
        forward(s, e, 0)

    def forward_chunk(s):
        for k in range(1, ex):
            owner = lax.rem(e + k, ex)
            ref = rows.at[s, pl.ds(1, dp - 1), :, block(t * ex + owner)]
            remote(ref, ref, x_s.at[s, k], x_r.at[s, k], at_ex(k)).wait_recv()
            forward(s, owner, k)

    def sibling_wait(s):
        for j in range(1, tn):
            for k in range(ex):
                other = lax.rem(t + j, tn) * ex + lax.rem(e + k, ex)
                ref = rows.at[s, pl.ds(1, dp - 1), :, block(other)]
                remote(ref, ref, f_s.at[s, k, j], f_r.at[s, k, j], at_tn(j)).wait_recv()

    n_h = hidden // h_tile

    def hid_copy(n, j):
        ref = hid.at[t, :, pl.ds(pl.multiple_of(n * h_tile, LANES), h_tile)]
        return remote(ref, ref, h_s.at[j, n], h_r.at[tn - j, n], at_tn(j))

    def compute(s):
        wait_chunk(s)
        last = s == chunks - 1

        @pl.loop(0, n_h)
        def _(n):
            at = pl.ds(pl.multiple_of(n * h_tile, LANES), h_tile)
            x = rows[s].reshape(dp * cap, depth)
            a = jnp.dot(x, wg[s % slots, :, at], preferred_element_type=F32)
            b = jnp.dot(x, wu[s % slots, :, at], preferred_element_type=F32)
            if s > 0:
                a = a + acc_g[:, at]
                b = b + acc_u[:, at]
            if last:
                hid[t, :, at] = (a / (1.0 + jnp.exp(-a)) * b).astype(BF16)
                for j in range(1, tn):
                    hid_copy(n, j).start()
            else:
                acc_g[:, at] = a
                acc_u[:, at] = b

    pack_chunk(0)
    for s in range(chunks):
        forward_chunk(s)
        if s + 1 < chunks:
            pack_chunk(s + 1)
        sibling_wait(s)
        compute(s)
        if s + slots < chunks:
            load_chunk(s + slots)

    for j in range(1, tn):
        other = lax.rem(t + j, tn)

        @pl.loop(0, n_h)
        def _(n):
            ref = hid.at[other, :, pl.ds(pl.multiple_of(n * h_tile, LANES), h_tile)]
            remote(ref, ref, h_s.at[j, n], h_r.at[j, n], at_tn(j)).wait_recv()

    for i in range(ex):
        k = (i + 1) % ex
        down_copy(i).wait()

        @pl.loop(0, piece // p_tile)
        def _(n):
            at = pl.ds(pl.multiple_of(n * p_tile, LANES), p_tile)
            y = jnp.zeros((dp * cap, p_tile), F32)
            for j in range(tn):
                y = y + jnp.dot(
                    hid[j], wd[i % d_slots, j * hidden:(j + 1) * hidden, at], preferred_element_type=F32
                )
            y = y.astype(BF16).reshape(dp, cap, p_tile)
            if k:
                dn_out[k - 1, :, :, at] = y
            else:
                dn_in[:, e, :, at] = y

        if k:
            send(dn_out.at[k - 1], dn_in.at[:, e], n_s.at[k], n_r.at[ex - k], at_ex(k))
        if i + d_slots < ex:
            down_copy(i + d_slots).start()
    for k in range(1, ex):
        ref = dn_in.at[:, lax.rem(e + k, ex)]
        remote(ref, ref, n_s.at[k], n_r.at[k], at_ex(k)).wait_recv()

    slot_id = lax.broadcasted_iota(jnp.int32, (group, ex * cap), 1).astype(F32)
    own_mix = None
    for i in range(dp):
        d = (i + 1) % dp
        m = jnp.transpose(meta[d])
        w = jnp.where(slot_id == m[:, 2:3], m[:, 0:1], 0.0)
        w = w + jnp.where(slot_id == m[:, 3:4], m[:, 1:2], 0.0)
        y = jnp.dot(
            w.astype(BF16), dn_in[d].reshape(ex * cap, piece), preferred_element_type=F32
        ).astype(BF16)
        if d:
            mix_out[d - 1] = y
            send(mix_out.at[d - 1], mix_in.at[dp - d], m_s.at[d], m_r.at[dp - d], at_dp(d))
        else:
            mix_in[0] = y
    for d in range(1, dp):
        remote(mix_in.at[d], mix_in.at[d], m_s.at[d], m_r.at[d], at_dp(d)).wait_recv()
    for x in range(ex):
        total = jnp.zeros((count, piece), F32)
        for d in range(dp):
            total = total + mix_in[d, x * count:(x + 1) * count, :].astype(F32)
        tr_out[x] = total.astype(BF16)
    for k in range(1, ex):
        send(tr_out.at[lax.rem(e + k, ex)], tr_in.at[e], t_s.at[k], t_r.at[ex - k], at_ex(k))
    tr_in[e] = tr_out[e]
    for k in range(1, ex):
        ref = tr_in.at[lax.rem(e + k, ex)]
        remote(ref, ref, t_s.at[k], t_r.at[k], at_ex(k)).wait_recv()

    score = jnp.zeros((count, 1), F32)
    own_rows = pl.ds(pl.multiple_of(e * count, 16), count)
    for x in range(ex):
        cols = pl.ds(pl.multiple_of(t * half + x * piece, LANES), piece)
        mixed = tokens[own_rows, cols].astype(F32) + tr_in[x].astype(F32)
        out[:, x * piece:(x + 1) * piece] = mixed.astype(BF16)
        lab = label[:, x * piece:(x + 1) * piece].astype(F32)
        score = score + jnp.sum(mixed * lab, axis=1, keepdims=True)
    part = jnp.sum(member[own_rows, :] * score, axis=0, keepdims=True)
    sc_out[...] = jnp.broadcast_to(part, (8, LANES))
    pairs = [(k, j) for k in range(ex) for j in range(tn) if k or j]
    for k, j in pairs:
        back = ((ex - k) % ex) * tn + (tn - j) % tn
        dev = (g, lax.rem(e + k, ex), lax.rem(t + j, tn))
        send(sc_out, sc_in.at[back], c_s.at[k * tn + j], c_r.at[back], dev)
    seq = sc_out[...]
    for k, j in pairs:
        n = k * tn + j
        dev = (g, lax.rem(e + k, ex), lax.rem(t + j, tn))
        remote(sc_out, sc_in.at[n], c_s.at[n], c_r.at[n], dev).wait_recv()
        seq = seq + sc_in[n]
    totals[...] = seq

    for c in sent:
        c.wait_send()
    for j in range(1, tn):

        @pl.loop(0, n_h)
        def _(n):
            hid_copy(n, j).wait_send()


def body(
    mesh_shape, tokens, norm_gain, expert_ids, gate_weights, w_gate, w_up, w_down,
    label_rows, seg_ids, pair_slot, ref_scores,
):
    group, width = tokens.shape
    hidden = w_gate.shape[2]
    size = dims(mesh_shape, group, width, hidden)
    dp, ex, tn, cap, piece, chunks, sub, h_tile, p_tile = size
    depth = ex * tn * sub
    slots = min(chunks, 2)
    d_slots = min(ex, 2)
    count = group // ex
    half = width // tn
    n_h = hidden // h_tile
    meta = jnp.concatenate(
        [gate_weights.T, expert_ids.T.astype(F32), jnp.zeros((4, group), F32)], axis=0
    )
    member = (seg_ids[0][:, None] == jnp.arange(LANES, dtype=jnp.int32)[None, :]).astype(F32)
    vm = pl.BlockSpec(memory_space=pltpu.VMEM)
    hbm = pl.BlockSpec(memory_space=pl.ANY)
    dma = pltpu.SemaphoreType.DMA
    scratch = [
        pltpu.VMEM((group, width), BF16),
        pltpu.VMEM((dp, 8, group), F32),
        pltpu.VMEM((chunks, dp, group, sub), BF16),
        pltpu.VMEM((chunks, ex, dp - 1, cap, sub), BF16),
        pltpu.VMEM((chunks, dp, cap, depth), BF16),
        pltpu.VMEM((slots, depth, hidden), BF16),
        pltpu.VMEM((slots, depth, hidden), BF16),
        pltpu.VMEM((d_slots, w_down.shape[1], piece), BF16),
        pltpu.VMEM((dp * cap, hidden), F32),
        pltpu.VMEM((dp * cap, hidden), F32),
        pltpu.VMEM((tn, dp * cap, hidden), BF16),
        pltpu.VMEM((ex - 1, dp, cap, piece), BF16),
        pltpu.VMEM((dp, ex, cap, piece), BF16),
        pltpu.VMEM((dp - 1, group, piece), BF16),
        pltpu.VMEM((dp, group, piece), BF16),
        pltpu.VMEM((ex, count, piece), BF16),
        pltpu.VMEM((ex, count, piece), BF16),
        pltpu.VMEM((8, LANES), F32),
        pltpu.VMEM((ex * tn, 8, LANES), F32),
        dma((2, chunks)), dma((ex,)),
        dma((dp,)), dma((dp,)),
        dma((chunks, dp)), dma((chunks, dp)),
        dma((chunks, ex)), dma((chunks, ex)),
        dma((chunks, ex, tn)), dma((chunks, ex, tn)),
        dma((tn, n_h)), dma((tn, n_h)),
        dma((ex,)), dma((ex,)),
        dma((dp,)), dma((dp,)),
        dma((ex,)), dma((ex,)),
        dma((ex * tn,)), dma((ex * tn,)),
    ]
    layer_out, totals = pl.pallas_call(
        functools.partial(kernel, size),
        out_shape=(
            jax.ShapeDtypeStruct((count, half), BF16),
            jax.ShapeDtypeStruct((8, LANES), F32),
        ),
        in_specs=[vm, vm, vm, vm, vm, hbm, hbm, hbm],
        out_specs=(vm, vm),
        scratch_shapes=scratch,
        compiler_params=pltpu.CompilerParams(
            collective_id=0, has_side_effects=True, vmem_limit_bytes=66_000_000
        ),
    )(tokens, norm_gain[None, :], meta, label_rows, member, w_gate, w_up, w_down)
    seq_totals = totals[0, :SEQS]
    slots_here = pair_slot[0]
    polarity = (1 - 2 * (slots_here % 2)).astype(F32)
    pair_member = (
        (slots_here // 2)[:, None] == jnp.arange(PAIRS, dtype=jnp.int32)[None, :]
    ).astype(F32)
    margins = dpo_beta * jnp.sum(
        pair_member * (polarity * (seq_totals - ref_scores[0]))[:, None], axis=0
    )
    return (layer_out, margins[None, :])


def solution(mesh):
    placed = (
        P("dp", None),
        P(),
        P("dp", None),
        P("dp", None),
        P("expert", None, ("dp", "tensor")),
        P("expert", None, ("dp", "tensor")),
        P("expert", "dp", "tensor"),
        P(("dp", "expert"), "tensor"),
        P("dp", None),
        P("dp", None),
        P("dp", None),
    )
    mesh_shape = tuple(mesh.shape[name] for name in ("dp", "expert", "tensor"))
    return jax.shard_map(
        functools.partial(body, mesh_shape),
        mesh=mesh,
        in_specs=placed,
        out_specs=(P(("dp", "expert"), "tensor"), P("dp", None)),
        check_vma=False,
    )
```

time: 209 us -> 107 us (0.51)
  the two profiles are of different devices: /device:TPU:0 before, /device:TPU:25 now
where the time goes in v1:
time: 107 us; the launch traced here: 106 us
  Pallas kernels  99.2 us (93%)
  other arithmetic  4.72 us (4%)
  local copies, waits for them, and re-layouts  1.7 us (2%)
    pallas_call x1, Pallas kernels, body(): pl.pallas_call(functools.partial(kernel, size), out_shape=(jax.ShapeDtype...  99.2 us

profile of v1, /device:TPU:25, one launch (start us, length us, event | category | flops | bytes accessed | tf_op | source)
XLA Modules:
  0.0 106.3 jit_solution(3768926669553647188)
XLA Ops:
  0.6 1.4 %fusion.member = f32[128,128]{1,0:T(8,128)} fusion(s32[128]{0:T(128)} %bitcast.26), kind=kLoop, calls=%fused_computation.1 | loop fusion | flops 32768 | bytes 66048 | tf_op jit(solution)/shard_map/convert_element_type | solution.py:348
  2.0 0.7 convert_bitcast_fusion
  2.7 0.1 pad.2.clone
  2.8 1.3 %maximum_maximum_fusion.meta_in = f32[8,128]{1,0:T(8,128)} fusion(f32[2,128]{1,0:T(2,128)S(1)} %convert_bitcast_fusion, f32[2,128]{1,0:T(2,128)} %bitcast.25, f32[8]{0:T(128)S(1)} %pad.2.clone), kind=kLoop, calls=%fused_computation.2 | loop fusion | flops 2048 | bytes 6176 | tf_op jit(solution)/shard_map/concatenate | solution.py:345
  4.1 0.0 copy-start
  4.1 0.0 copy-start.1
  4.1 99.2 %shard_map.122 = (bf16[32,3072]{1,0:T(8,128)(2,1)}, f32[8,128]{1,0:T(8,128)}) custom-call(bf16[128,6144]{1,0:T(8,128)(2,1)} %tokens.1, f32[1,6144]{1,0:T(1,128)} %bitcast.24, f32[8,128]{1,0:T(8,128)} %maximum_maximum_fusion.meta_in, bf16[32,3072]{1,0:T(8,128)(2,1)} %label.1, f32[128,128]{1,0:T(8,128)} %fusion.member, bf16[1,6144,1536]{2,1,0:T(8,128)(2,1)} %w_gate.1, ...), custom_call_target="tpu_custom_call" | custom-call | tf_op jit(solution)/shard_map/pallas_call | solution.py:383
  103.3 0.0 copy-done
  103.3 0.0 copy-done.1
  103.3 0.7 fusion.5
  104.0 0.1 fusion.1
  104.2 0.5 multiply_bitcast_fusion
  104.7 1.6 %copy.14 = bf16[32,3072]{1,0:T(8,128)(2,1)} copy(bf16[32,3072]{1,0:T(8,128)(2,1)} %get-tuple-element.8) | data formatting | bytes 393216
  (2 shorter events, 0.0 us)
Async XLA Ops:
  4.1 99.2 %copy-start = (f32[1,4]{1,0:T(1,128)S(1)}, f32[1,4]{1,0:T(1,128)}, u32[]{:S(2)}) copy-start(f32[1,4]{1,0:T(1,128)} %param.21) | copy-start | bytes 52
  4.1 99.2 %copy-start.1 = (s32[1,4]{1,0:T(1,128)S(1)}, s32[1,4]{1,0:T(1,128)}, u32[]{:S(2)}) copy-start(s32[1,4]{1,0:T(1,128)} %param.20) | copy-start | bytes 52

commit v2 on v1

--- a/solution.py
+++ b/solution.py
@@ -25,19 +25,18 @@
     chunks = 3 if piece % 384 == 0 else 1
     sub = piece // chunks
     h_tile = 256 if hidden % 256 == 0 else 128
-    p_tile = 256 if piece % 256 == 0 else 128
-    return dp, ex, tn, cap_pad, piece, chunks, sub, h_tile, p_tile
+    return dp, ex, tn, cap_pad, piece, chunks, sub, h_tile
 
 
 def kernel(
-    size, tokens, gain, meta_in, label, member, w_gate, w_up, w_down,
+    size, tokens, gain, meta_in, label, w_gate, w_up, w_down,
     out, totals,
     normed, meta, tok, pack, rows, wg, wu, wd, acc_g, acc_u, hid, dn_out, dn_in,
-    mix_out, mix_in, tr_out, tr_in, sc_out, sc_in,
+    mix_out, mix_in, mixing, member, tr_out, tr_in, sc_out, sc_in,
     w_sem, d_sem, meta_s, meta_r, z_s, z_r, x_s, x_r, f_s, f_r, h_s, h_r,
     n_s, n_r, m_s, m_r, t_s, t_r, c_s, c_r,
 ):
-    dp, ex, tn, cap, piece, chunks, sub, h_tile, p_tile = size
+    dp, ex, tn, cap, piece, chunks, sub, h_tile = size
     group, width = tokens.shape
     half = width // tn
     hidden = w_gate.shape[2]
@@ -45,7 +44,9 @@
     count = group // ex
     g, e, t = lax.axis_index("dp"), lax.axis_index("expert"), lax.axis_index("tensor")
     slots = min(chunks, 2)
+    window = 1
     d_slots = wd.shape[0]
+    n_down = chunks * ex
     sent = []
 
     def at_dp(k):
@@ -81,9 +82,9 @@
             pltpu.make_async_copy(src.at[0, pl.ds(0, depth)], dst.at[s % slots], w_sem.at[i, s]).wait()
 
     def down_copy(i):
-        owner = lax.rem(e + i + 1, ex)
+        start = lax.rem(e + i + 1, ex) * piece + (i // ex) * sub
         return pltpu.make_async_copy(
-            w_down.at[0, :, pl.ds(pl.multiple_of(owner * piece, LANES), piece)],
+            w_down.at[0, :, pl.ds(pl.multiple_of(start, LANES), sub)],
             wd.at[i % d_slots],
             d_sem.at[i],
         )
@@ -135,13 +136,17 @@
     my_col = pl.multiple_of(t * half + e * piece, LANES)
     for k in range(1, dp):
         send(meta.at[0], meta.at[dp - k], meta_s.at[k], meta_r.at[dp - k], at_dp(k))
-    for s in range(chunks):
+
+    def send_tokens(s):
         for k in range(1, dp):
             send(
                 normed.at[:, pl.ds(pl.multiple_of(my_col + s * sub, LANES), sub)],
                 tok.at[s, dp - k],
                 z_s.at[s, k], z_r.at[s, dp - k], at_dp(k),
             )
+
+    for s in range(min(chunks, window)):
+        send_tokens(s)
 
     row_id = lax.broadcasted_iota(jnp.int32, (cap, group), 0).astype(F32) + (e * cap).astype(F32)
     own_hot = jnp.where((row_id == s0) | (row_id == s1), 1.0, 0.0).astype(BF16)
@@ -174,6 +179,8 @@
             for x in range(ex):
                 pack[s, x, d - 1] = got[x]
             rows[s, d, :, block(mine)] = pack[s, e, d - 1]
+        if s + window < chunks:
+            send_tokens(s + window)
         for k in range(1, ex):
             send(
                 pack.at[s, lax.rem(e + k, ex)],
@@ -241,69 +248,78 @@
             ref = hid.at[other, :, pl.ds(pl.multiple_of(n * h_tile, LANES), h_tile)]
             remote(ref, ref, h_s.at[j, n], h_r.at[j, n], at_tn(j)).wait_recv()
 
-    for i in range(ex):
-        k = (i + 1) % ex
+    for i in range(n_down):
+        c, k = i // ex, (i + 1) % ex
         down_copy(i).wait()
-
-        @pl.loop(0, piece // p_tile)
-        def _(n):
-            at = pl.ds(pl.multiple_of(n * p_tile, LANES), p_tile)
-            y = jnp.zeros((dp * cap, p_tile), F32)
-            for j in range(tn):
-                y = y + jnp.dot(
-                    hid[j], wd[i % d_slots, j * hidden:(j + 1) * hidden, at], preferred_element_type=F32
-                )
-            y = y.astype(BF16).reshape(dp, cap, p_tile)
-            if k:
-                dn_out[k - 1, :, :, at] = y
-            else:
-                dn_in[:, e, :, at] = y
-
+        y = jnp.zeros((dp * cap, sub), F32)
+        for j in range(tn):
+            y = y + jnp.dot(
+                hid[j], wd[i % d_slots, j * hidden:(j + 1) * hidden, :], preferred_element_type=F32
+            )
+        y = y.astype(BF16).reshape(dp, cap, sub)
         if k:
-            send(dn_out.at[k - 1], dn_in.at[:, e], n_s.at[k], n_r.at[ex - k], at_ex(k))
-        if i + d_slots < ex:
+            dn_out[c, k - 1] = y
+            send(dn_out.at[c, k - 1], dn_in.at[c, :, e], n_s.at[c, k], n_r.at[c, ex - k], at_ex(k))
+        else:
+            dn_in[c, :, e] = y
+        if i + d_slots < n_down:
             down_copy(i + d_slots).start()
-    for k in range(1, ex):
-        ref = dn_in.at[:, lax.rem(e + k, ex)]
-        remote(ref, ref, n_s.at[k], n_r.at[k], at_ex(k)).wait_recv()
 
     slot_id = lax.broadcasted_iota(jnp.int32, (group, ex * cap), 1).astype(F32)
-    own_mix = None
-    for i in range(dp):
-        d = (i + 1) % dp
+    for d in range(dp):
         m = jnp.transpose(meta[d])
         w = jnp.where(slot_id == m[:, 2:3], m[:, 0:1], 0.0)
         w = w + jnp.where(slot_id == m[:, 3:4], m[:, 1:2], 0.0)
-        y = jnp.dot(
-            w.astype(BF16), dn_in[d].reshape(ex * cap, piece), preferred_element_type=F32
-        ).astype(BF16)
-        if d:
-            mix_out[d - 1] = y
-            send(mix_out.at[d - 1], mix_in.at[dp - d], m_s.at[d], m_r.at[dp - d], at_dp(d))
-        else:
-            mix_in[0] = y
-    for d in range(1, dp):
-        remote(mix_in.at[d], mix_in.at[d], m_s.at[d], m_r.at[d], at_dp(d)).wait_recv()
-    for x in range(ex):
-        total = jnp.zeros((count, piece), F32)
-        for d in range(dp):
-            total = total + mix_in[d, x * count:(x + 1) * count, :].astype(F32)
-        tr_out[x] = total.astype(BF16)
-    for k in range(1, ex):
-        send(tr_out.at[lax.rem(e + k, ex)], tr_in.at[e], t_s.at[k], t_r.at[ex - k], at_ex(k))
-    tr_in[e] = tr_out[e]
-    for k in range(1, ex):
-        ref = tr_in.at[lax.rem(e + k, ex)]
-        remote(ref, ref, t_s.at[k], t_r.at[k], at_ex(k)).wait_recv()
+        mixing[d] = w.astype(BF16)
+        if d == 0:
+            seq_id = lax.broadcasted_iota(jnp.int32, (group, LANES), 1).astype(F32)
+            member[...] = jnp.where(seq_id == m[:, 4:5], 1.0, 0.0)
+    for c in range(chunks):
+        for k in range(1, ex):
+            ref = dn_in.at[c, :, lax.rem(e + k, ex)]
+            remote(ref, ref, n_s.at[c, k], n_r.at[c, k], at_ex(k)).wait_recv()
+        for i in range(dp):
+            d = (i + 1) % dp
+            y = jnp.dot(
+                mixing[d], dn_in[c, d].reshape(ex * cap, sub), preferred_element_type=F32
+            ).astype(BF16)
+            if d:
+                mix_out[c, d - 1] = y
+                send(
+                    mix_out.at[c, d - 1], mix_in.at[c, dp - d],
+                    m_s.at[c, d], m_r.at[c, dp - d], at_dp(d),
+                )
+            else:
+                mix_in[c, 0] = y
+    for c in range(chunks):
+        for d in range(1, dp):
+            ref = mix_in.at[c, d]
+            remote(ref, ref, m_s.at[c, d], m_r.at[c, d], at_dp(d)).wait_recv()
+        for x in range(ex):
+            total = jnp.zeros((count, sub), F32)
+            for d in range(dp):
+                total = total + mix_in[c, d, x * count:(x + 1) * count, :].astype(F32)
+            tr_out[c, x] = total.astype(BF16)
+        for k in range(1, ex):
+            send(
+                tr_out.at[c, lax.rem(e + k, ex)], tr_in.at[c, e],
+                t_s.at[c, k], t_r.at[c, ex - k], at_ex(k),
+            )
+        tr_in[c, e] = tr_out[c, e]
 
     score = jnp.zeros((count, 1), F32)
     own_rows = pl.ds(pl.multiple_of(e * count, 16), count)
-    for x in range(ex):
-        cols = pl.ds(pl.multiple_of(t * half + x * piece, LANES), piece)
-        mixed = tokens[own_rows, cols].astype(F32) + tr_in[x].astype(F32)
-        out[:, x * piece:(x + 1) * piece] = mixed.astype(BF16)
-        lab = label[:, x * piece:(x + 1) * piece].astype(F32)
-        score = score + jnp.sum(mixed * lab, axis=1, keepdims=True)
+    for c in range(chunks):
+        for k in range(1, ex):
+            ref = tr_in.at[c, lax.rem(e + k, ex)]
+            remote(ref, ref, t_s.at[c, k], t_r.at[c, k], at_ex(k)).wait_recv()
+        for x in range(ex):
+            low = x * piece + c * sub
+            cols = pl.ds(pl.multiple_of(t * half + low, LANES), sub)
+            mixed = tokens[own_rows, cols].astype(F32) + tr_in[c, x].astype(F32)
+            out[:, low:low + sub] = mixed.astype(BF16)
+            lab = label[:, low:low + sub].astype(F32)
+            score = score + jnp.sum(mixed * lab, axis=1, keepdims=True)
     part = jnp.sum(member[own_rows, :] * score, axis=0, keepdims=True)
     sc_out[...] = jnp.broadcast_to(part, (8, LANES))
     pairs = [(k, j) for k in range(ex) for j in range(tn) if k or j]
@@ -335,17 +351,16 @@
     group, width = tokens.shape
     hidden = w_gate.shape[2]
     size = dims(mesh_shape, group, width, hidden)
-    dp, ex, tn, cap, piece, chunks, sub, h_tile, p_tile = size
+    dp, ex, tn, cap, piece, chunks, sub, h_tile = size
     depth = ex * tn * sub
     slots = min(chunks, 2)
-    d_slots = min(ex, 2)
+    d_slots = min(chunks * ex, 2 * chunks)
     count = group // ex
     half = width // tn
     n_h = hidden // h_tile
     meta = jnp.concatenate(
-        [gate_weights.T, expert_ids.T.astype(F32), jnp.zeros((4, group), F32)], axis=0
+        [gate_weights.T, expert_ids.T.astype(F32), seg_ids.astype(F32), jnp.zeros((3, group), F32)], axis=0
     )
-    member = (seg_ids[0][:, None] == jnp.arange(LANES, dtype=jnp.int32)[None, :]).astype(F32)
     vm = pl.BlockSpec(memory_space=pltpu.VMEM)
     hbm = pl.BlockSpec(memory_space=pl.ANY)
     dma = pltpu.SemaphoreType.DMA
@@ -357,27 +372,29 @@
         pltpu.VMEM((chunks, dp, cap, depth), BF16),
         pltpu.VMEM((slots, depth, hidden), BF16),
         pltpu.VMEM((slots, depth, hidden), BF16),
-        pltpu.VMEM((d_slots, w_down.shape[1], piece), BF16),
+        pltpu.VMEM((d_slots, w_down.shape[1], sub), BF16),
         pltpu.VMEM((dp * cap, hidden), F32),
         pltpu.VMEM((dp * cap, hidden), F32),
         pltpu.VMEM((tn, dp * cap, hidden), BF16),
-        pltpu.VMEM((ex - 1, dp, cap, piece), BF16),
-        pltpu.VMEM((dp, ex, cap, piece), BF16),
-        pltpu.VMEM((dp - 1, group, piece), BF16),
-        pltpu.VMEM((dp, group, piece), BF16),
-        pltpu.VMEM((ex, count, piece), BF16),
-        pltpu.VMEM((ex, count, piece), BF16),
+        pltpu.VMEM((chunks, ex - 1, dp, cap, sub), BF16),
+        pltpu.VMEM((chunks, dp, ex, cap, sub), BF16),
+        pltpu.VMEM((chunks, dp - 1, group, sub), BF16),
+        pltpu.VMEM((chunks, dp, group, sub), BF16),
+        pltpu.VMEM((dp, group, ex * cap), BF16),
+        pltpu.VMEM((group, LANES), F32),
+        pltpu.VMEM((chunks, ex, count, sub), BF16),
+        pltpu.VMEM((chunks, ex, count, sub), BF16),
         pltpu.VMEM((8, LANES), F32),
         pltpu.VMEM((ex * tn, 8, LANES), F32),
-        dma((2, chunks)), dma((ex,)),
+        dma((2, chunks)), dma((chunks * ex,)),
         dma((dp,)), dma((dp,)),
         dma((chunks, dp)), dma((chunks, dp)),
         dma((chunks, ex)), dma((chunks, ex)),
         dma((chunks, ex, tn)), dma((chunks, ex, tn)),
         dma((tn, n_h)), dma((tn, n_h)),
-        dma((ex,)), dma((ex,)),
-        dma((dp,)), dma((dp,)),
-        dma((ex,)), dma((ex,)),
+        dma((chunks, ex)), dma((chunks, ex)),
+        dma((chunks, dp)), dma((chunks, dp)),
+        dma((chunks, ex)), dma((chunks, ex)),
         dma((ex * tn,)), dma((ex * tn,)),
     ]
     layer_out, totals = pl.pallas_call(
@@ -386,13 +403,13 @@
             jax.ShapeDtypeStruct((count, half), BF16),
             jax.ShapeDtypeStruct((8, LANES), F32),
         ),
-        in_specs=[vm, vm, vm, vm, vm, hbm, hbm, hbm],
+        in_specs=[vm, vm, vm, vm, hbm, hbm, hbm],
         out_specs=(vm, vm),
         scratch_shapes=scratch,
         compiler_params=pltpu.CompilerParams(
             collective_id=0, has_side_effects=True, vmem_limit_bytes=66_000_000
         ),
-    )(tokens, norm_gain[None, :], meta, label_rows, member, w_gate, w_up, w_down)
+    )(tokens, norm_gain[None, :], meta, label_rows, w_gate, w_up, w_down)
     seq_totals = totals[0, :SEQS]
     slots_here = pair_slot[0]
     polarity = (1 - 2 * (slots_here % 2)).astype(F32)

time: 107 us -> 92.7 us (0.87)
  the two profiles are of different devices: /device:TPU:25 before, /device:TPU:0 now
where the time goes in v2:
time: 92.7 us; the launch traced here: 92.5 us
  Pallas kernels  86.1 us (93%)
  other arithmetic  4.01 us (4%)
  local copies, waits for them, and re-layouts  1.7 us (2%)
    pallas_call x1, Pallas kernels, body(): pl.pallas_call(functools.partial(kernel, size), out_shape=(jax.ShapeDtype...  86.1 us

profile of v2, /device:TPU:0, one launch (start us, length us, event | category | flops | bytes accessed | tf_op | source)
XLA Modules:
  0.0 92.5 jit_solution(8305480819778736669)
XLA Ops:
  0.6 0.7 convert_bitcast_fusion
  1.3 0.1 pad.3.clone
  1.4 0.7 convert_element_type.19
  2.0 1.3 %maximum_maximum_fusion.meta_in = f32[8,128]{1,0:T(8,128)} fusion(f32[1,128]{1,0:T(1,128)S(1)} %convert_element_type.19, f32[2,128]{1,0:T(2,128)S(1)} %convert_bitcast_fusion, f32[2,128]{1,0:T(2,128)} %bitcast.24, f32[8]{0:T(128)S(1)} %pad.3.clone), kind=kLoop, calls=%fused_computation | loop fusion | flops 3072 | bytes 6688 | tf_op jit(solution)/shard_map/concatenate | solution.py:361
  3.4 0.0 copy-start
  3.4 0.0 copy-start.1
  3.4 86.1 %shard_map.122 = (bf16[32,3072]{1,0:T(8,128)(2,1)}, f32[8,128]{1,0:T(8,128)}) custom-call(bf16[128,6144]{1,0:T(8,128)(2,1)} %tokens.1, f32[1,6144]{1,0:T(1,128)} %bitcast.23, f32[8,128]{1,0:T(8,128)} %maximum_maximum_fusion.meta_in, bf16[32,3072]{1,0:T(8,128)(2,1)} %label.1, bf16[1,6144,1536]{2,1,0:T(8,128)(2,1)} %w_gate.1, bf16[1,6144,1536]{2,1,0:T(8,128)(2,1)} %w_up.1, ...), custom_call_target="tpu_custom_call" | custom-call | tf_op jit(solution)/shard_map/pallas_call | solution.py:400
  89.5 0.0 copy-done
  89.5 0.0 copy-done.1
  89.5 0.7 fusion.4
  90.2 0.1 fusion
  90.3 0.5 multiply_bitcast_fusion
  90.9 1.6 %copy.14 = bf16[32,3072]{1,0:T(8,128)(2,1)} copy(bf16[32,3072]{1,0:T(8,128)(2,1)} %get-tuple-element.8) | data formatting | bytes 393216
  (2 shorter events, 0.0 us)
Async XLA Ops:
  3.4 86.1 %copy-start = (f32[1,4]{1,0:T(1,128)S(1)}, f32[1,4]{1,0:T(1,128)}, u32[]{:S(2)}) copy-start(f32[1,4]{1,0:T(1,128)} %param.21) | copy-start | bytes 52
  3.4 86.1 %copy-start.1 = (s32[1,4]{1,0:T(1,128)S(1)}, s32[1,4]{1,0:T(1,128)}, u32[]{:S(2)}) copy-start(s32[1,4]{1,0:T(1,128)} %param.20) | copy-start | bytes 52
